TPU v7x, 32 devices: a whole 2x2x4 slice. The times are simulated.
32 devices in a mesh: cond: 4 (over y, x), space: 8 (over z, core).
Axes of the slice: x: 2, y: 2, z: 4, core: 2. Of those that a mesh axis runs over, the one named last changes fastest.
Arguments:
- flow: float32 [8, 3, 128, 2048], P('cond', None, 'space'), may hold values from -4 to 4
- forcing: float32 [8, 2, 128, 2048], P('cond', None, 'space'), may hold values from -4 to 4
- wet: int32 [8, 128, 2048], P('cond', 'space'), may hold values 0 or 1
- depth: float32 [128, 2048], P('space'), may hold values from 0.5 to 2
- limiter: int32 [128, 2048], P('space'), may hold values 0 or 1
- weights: int32 [8], replicated, may hold values from 1 to 9
- bed: float32 [128, 2048], P('space'), may hold values from -6 to 6
- diffusivity: float32 [128, 2048], P('space'), may hold values from 0.2 to 5
Outputs:
- surface: float32 [8, 128, 2048], P('cond', 'space')
- bed_new: float32 [128, 2048], P('space')
All inputs are finite; a program needn't handle non-finite values. No bound on the sum of `wet` or of `limiter` on one device may be relied on, other than what follows from the above.
Results may differ from a plain program's by a relative error of at most 0.0001.
Values sent between devices are 32-bit elements; how exact they have to be, the bound alone decides.
No kernel may reach another device: no remote copies, remote signals or barrier semaphores. Data moves between devices by JAX's collectives and lax.ppermute only.
A program may use at most 64 MiB of HBM per device.

v0:
```python
import jax
import jax.numpy as jnp
from jax import lax
from jax.sharding import PartitionSpec as P

STEPS = 4
ITERS = 2
time_step = 0.4
gravity = 1.0
friction = 0.1
transport_base = 0.5
morph_factor = 1.0
slope_coeff = 1.0


def with_halo(cells, sides, width):
    for axis, dim in sides:
        count = lax.axis_size(axis)
        ends = count - 1
        head = lax.slice_in_dim(cells, 0, width, axis=dim)
        tail = lax.slice_in_dim(cells, cells.shape[dim] - width, cells.shape[dim], axis=dim)
        cells = jnp.concatenate(
            [
                lax.ppermute(tail, axis, [(i, (i + 1) % count) for i in range(ends)]),
                cells,
                lax.ppermute(head, axis, [((i + 1) % count, i) for i in range(ends)]),
            ],
            axis=dim,
        )
    return cells


def rows_diff(padded):
    return 0.5 * (padded[..., 2:, :] - padded[..., :-2, :])


def column_diff(field):
    padded = jnp.pad(field, [(0, 0)] * (field.ndim - 1) + [(1, 1)])
    return 0.5 * (padded[..., 2:] - padded[..., :-2])


def paired_fields(state_now, depth):
    return [state_now[:, 0], depth * state_now[:, 1]]


def flow_rim(state_now, depth):
    paired = jnp.stack(paired_fields(state_now, depth), 1)
    return with_halo(paired, (("space", 2),), 1)


def tendency(state_now, rim_rows, depth, wet_mask, force):
    elevation, vel_first, vel_second = (state_now[:, 0], state_now[:, 1], state_now[:, 2])
    rate_elev = -(rows_diff(rim_rows[:, 1]) + column_diff(depth * vel_second))
    rate_first = -gravity * rows_diff(rim_rows[:, 0]) - friction * vel_first + force[:, 0]
    rate_second = -gravity * column_diff(elevation) - friction * vel_second + force[:, 1]
    return wet_mask * jnp.stack([rate_elev, rate_first, rate_second], 1)


def transport(state_now, limit_mask):
    vel_first, vel_second = (state_now[:, 1], state_now[:, 2])
    energy = vel_first * vel_first + vel_second * vel_second
    factor = (transport_base + energy) / (1.0 + limit_mask * energy)
    return (vel_first * factor, vel_second * factor)


def second_section(state_now, rim_rows, depth, wet_mask, forcing):
    first_section = state_now + time_step * tendency(state_now, rim_rows, depth, wet_mask, forcing)
    rim_next = flow_rim(first_section, depth)
    return 0.5 * (
        state_now
        + first_section
        + time_step * tendency(first_section, rim_next, depth, wet_mask, forcing)
    )


def rim_cells(field):
    padded = with_halo(field, (("space", 0),), 1)
    return jnp.pad(padded, ((0, 0), (1, 1)))


def reduce_all(values):
    return lax.psum(values, "space")


def neighbours(padded):
    return [padded[:-2, 1:-1], padded[2:, 1:-1], padded[1:-1, :-2], padded[1:-1, 2:]]


def apply_op(field, coefs):
    near = neighbours(rim_cells(field))
    total = coefs[0] * (field - near[0]) + coefs[1] * (field - near[1])
    total = total + coefs[2] * (field - near[2]) + coefs[3] * (field - near[3])
    return field + slope_coeff * total


def local(flow, forcing, wet, depth, limiter, weights, bed, diffusivity):
    cond_here = flow.shape[0]
    wet_mask = wet.astype(jnp.float32)[:, None]
    limit_mask = limiter.astype(jnp.float32)
    state_now = flow
    bed_change = jnp.zeros((cond_here,) + flow.shape[2:], jnp.float32)
    for stepper in range(STEPS):
        rim_rows = flow_rim(state_now, depth)
        state_now = second_section(state_now, rim_rows, depth, wet_mask, forcing)
        flux_first, flux_second = transport(state_now, limit_mask)
        flux_rows = with_halo(flux_first, (("space", 1),), 1)
        bed_change = bed_change - morph_factor * (rows_diff(flux_rows) + column_diff(flux_second))
    weight_all = weights.astype(jnp.float32)
    weight_mine = lax.dynamic_slice_in_dim(
        weight_all, lax.axis_index("cond") * cond_here, cond_here
    )
    own_part = jnp.sum(weight_mine[:, None, None] * bed_change, 0) / jnp.sum(weight_all)
    portion = lax.psum(own_part, "cond")
    padded = rim_cells(diffusivity)
    centre = padded[1:-1, 1:-1]
    coefs = [centre * other / (centre + other) for other in neighbours(padded)]
    rhs = bed + portion
    solution = jnp.zeros_like(rhs)
    image = apply_op(rhs, coefs)
    totals = reduce_all(jnp.stack([jnp.sum(rhs * rhs), jnp.sum(rhs * image)]))
    norm_now = totals[0]
    alpha = norm_now / totals[1]
    residual, direction, along = (rhs, rhs, image)
    for sweep in range(ITERS):
        solution = solution + alpha * direction
        if sweep + 1 < ITERS:
            residual = residual - alpha * along
            image = apply_op(residual, coefs)
            totals = reduce_all(
                jnp.stack([jnp.sum(residual * residual), jnp.sum(residual * image)])
            )
            ratio = totals[0] / norm_now
            alpha = totals[0] / (totals[1] - ratio * totals[0] / alpha)
            direction = residual + ratio * direction
            along = image + ratio * along
            norm_now = totals[0]
    return (state_now[:, 0], solution)


def solution(mesh):
    in_specs = (
        P("cond", None, "space", None),
        P("cond", None, "space", None),
        P("cond", "space", None),
        P("space", None),
        P("space", None),
        P(),
        P("space", None),
        P("space", None),
    )
    out_specs = (P("cond", "space", None), P("space", None))
    return jax.shard_map(local, mesh=mesh, in_specs=in_specs, out_specs=out_specs, check_vma=False)
```

profile of v0, /device:TPU:0, one launch (start us, length us, event | category | flops | bytes accessed | tf_op | source)
XLA Modules:
  0.0 204.6 jit_solution(7893001801209511206)
XLA Ops:
  7.2 1.2 fusion.205
  8.4 2.5 %collective-permute-start = (f32[2,2,1,2048]{3,2,0,1:T(1,128)S(1)}, f32[2,2,1,2048]{3,2,0,1:T(1,128)S(1)}, u32[]{:S(2)}, u32[]{:S(2)}) collective-permute-start(f32[2,2,1,2048]{3,2,0,1:T(1,128)S(1)} %get-tuple-element.99), channel_id=1, source_target_pairs={{0,1},{1,2},{2,3},{3,4},{4,5},{5,6},{6,7},{8,9},{9,10},{10,11},{11... | collective-permute-start | bytes 98312 | tf_op jit(solution)/shard_map/ppermute | solution.py:24
  11.0 1.3 collective-permute-start.1
  12.3 3.9 %collective-permute-done.1 = f32[2,2,1,2048]{3,2,0,1:T(1,128)S(1)} collective-permute-done((f32[2,2,1,2048]{3,2,0,1:T(1,128)S(1)}, f32[2,2,1,2048]{3,2,0,1:T(1,128)S(1)}, u32[]{:S(2)}, u32[]{:S(2)}) %collective-permute-start.1) | collective-permute-done | bytes 32800 | tf_op jit(solution)/shard_map/ppermute | solution.py:26
  16.5 1.0 copy-done
  18.3 4.5 %collective-permute-start.2 = (f32[2,2,1,2048]{3,2,0,1:T(1,128)S(1)}, f32[2,2,1,2048]{3,2,0,1:T(1,128)S(1)}, u32[]{:S(2)}, u32[]{:S(2)}) collective-permute-start(f32[2,2,1,2048]{3,2,0,1:T(1,128)S(1)} %get-tuple-element.97), channel_id=1, source_target_pairs={{0,1},{1,2},{2,3},{3,4},{4,5},{5,6},{6,7},{8,9},{9,10},{10,11},{11... | collective-permute-start | bytes 98312 | tf_op jit(solution)/shard_map/ppermute | solution.py:24
  22.9 1.3 collective-permute-start.3
  24.2 1.8 collective-permute-done.3
  27.0 4.1 %collective-permute-start.4 = (f32[2,2,1,2048]{3,2,0,1:T(1,128)S(1)}, f32[2,2,1,2048]{3,2,0,1:T(1,128)S(1)}, u32[]{:S(2)}, u32[]{:S(2)}) collective-permute-start(f32[2,2,1,2048]{3,2,0,1:T(1,128)S(1)} %get-tuple-element.95), channel_id=1, source_target_pairs={{0,1},{1,2},{2,3},{3,4},{4,5},{5,6},{6,7},{8,9},{9,10},{10,11},{11... | collective-permute-start | bytes 98312 | tf_op jit(solution)/shard_map/ppermute | solution.py:24
  31.0 1.3 collective-permute-start.5
  32.4 1.8 collective-permute-done.5
  35.2 4.1 %collective-permute-start.6 = (f32[2,2,1,2048]{3,2,0,1:T(1,128)S(1)}, f32[2,2,1,2048]{3,2,0,1:T(1,128)S(1)}, u32[]{:S(2)}, u32[]{:S(2)}) collective-permute-start(f32[2,2,1,2048]{3,2,0,1:T(1,128)S(1)} %get-tuple-element.93), channel_id=1, source_target_pairs={{0,1},{1,2},{2,3},{3,4},{4,5},{5,6},{6,7},{8,9},{9,10},{10,11},{11... | collective-permute-start | bytes 98312 | tf_op jit(solution)/shard_map/ppermute | solution.py:24
  39.3 1.3 collective-permute-start.7
  40.6 1.8 collective-permute-done.7
  43.6 4.1 %collective-permute-start.8 = (f32[2,2,1,2048]{3,2,0,1:T(1,128)S(1)}, f32[2,2,1,2048]{3,2,0,1:T(1,128)S(1)}, u32[]{:S(2)}, u32[]{:S(2)}) collective-permute-start(f32[2,2,1,2048]{3,2,0,1:T(1,128)S(1)} %get-tuple-element.91), channel_id=1, source_target_pairs={{0,1},{1,2},{2,3},{3,4},{4,5},{5,6},{6,7},{8,9},{9,10},{10,11},{11... | collective-permute-start | bytes 98312 | tf_op jit(solution)/shard_map/ppermute | solution.py:24
  47.6 1.3 collective-permute-start.9
  48.9 1.8 collective-permute-done.9
  52.1 4.1 %collective-permute-start.10 = (f32[2,2,1,2048]{3,2,0,1:T(1,128)S(1)}, f32[2,2,1,2048]{3,2,0,1:T(1,128)S(1)}, u32[]{:S(2)}, u32[]{:S(2)}) collective-permute-start(f32[2,2,1,2048]{3,2,0,1:T(1,128)S(1)} %get-tuple-element.89), channel_id=1, source_target_pairs={{0,1},{1,2},{2,3},{3,4},{4,5},{5,6},{6,7},{8,9},{9,10},{10,11},{11... | collective-permute-start | bytes 98312 | tf_op jit(solution)/shard_map/ppermute | solution.py:24
  56.1 1.3 collective-permute-start.11
  57.5 1.3 collective-permute-start.16
  58.8 3.7 %collective-permute-start.17 = (f32[2,1,2048]{2,1,0:T(1,128)S(1)}, f32[2,1,2048]{2,1,0:T(1,128)S(1)}, u32[]{:S(2)}, u32[]{:S(2)}) collective-permute-start(f32[2,1,2048]{2,1,0:T(1,128)S(1)} %get-tuple-element.102), channel_id=1, source_target_pairs={{0,1},{1,2},{2,3},{3,4},{4,5},{5,6},{6,7},{8,9},{9,10},{10,11},{11... | collective-permute-start | bytes 49160 | tf_op jit(solution)/shard_map/ppermute | solution.py:24
  63.9 3.6 %collective-permute-start.12 = (f32[2,2,1,2048]{3,2,0,1:T(1,128)S(1)}, f32[2,2,1,2048]{3,2,0,1:T(1,128)S(1)}, u32[]{:S(2)}, u32[]{:S(2)}) collective-permute-start(f32[2,2,1,2048]{3,2,0,1:T(1,128)S(1)} %get-tuple-element.87), channel_id=1, source_target_pairs={{0,1},{1,2},{2,3},{3,4},{4,5},{5,6},{6,7},{8,9},{9,10},{10,11},{11... | collective-permute-start | bytes 98312 | tf_op jit(solution)/shard_map/ppermute | solution.py:24
  67.5 1.3 collective-permute-start.13
  68.9 1.3 collective-permute-start.18
  72.1 4.1 %collective-permute-start.14 = (f32[2,2,1,2048]{3,2,0,1:T(1,128)S(1)}, f32[2,2,1,2048]{3,2,0,1:T(1,128)S(1)}, u32[]{:S(2)}, u32[]{:S(2)}) collective-permute-start(f32[2,2,1,2048]{3,2,0,1:T(1,128)S(1)} %get-tuple-element.85), channel_id=1, source_target_pairs={{0,1},{1,2},{2,3},{3,4},{4,5},{5,6},{6,7},{8,9},{9,10},{10,11},{11... | collective-permute-start | bytes 98312 | tf_op jit(solution)/shard_map/ppermute | solution.py:24
  76.2 1.3 collective-permute-start.15
  77.5 3.4 %collective-permute-start.19 = (f32[2,1,2048]{2,1,0:T(1,128)S(1)}, f32[2,1,2048]{2,1,0:T(1,128)S(1)}, u32[]{:S(2)}, u32[]{:S(2)}) collective-permute-start(f32[2,1,2048]{2,1,0:T(1,128)S(1)} %get-tuple-element.104), channel_id=1, source_target_pairs={{0,1},{1,2},{2,3},{3,4},{4,5},{5,6},{6,7},{8,9},{9,10},{10,11},{11... | collective-permute-start | bytes 49160 | tf_op jit(solution)/shard_map/ppermute | solution.py:24
  81.0 1.3 collective-permute-start.20
  82.9 0.9 fusion.19
  84.0 4.3 %collective-permute-start.21 = (f32[2,1,2048]{2,1,0:T(1,128)S(1)}, f32[2,1,2048]{2,1,0:T(1,128)S(1)}, u32[]{:S(2)}, u32[]{:S(2)}) collective-permute-start(f32[2,1,2048]{2,1,0:T(1,128)S(1)} %get-tuple-element.106), channel_id=1, source_target_pairs={{0,1},{1,2},{2,3},{3,4},{4,5},{5,6},{6,7},{8,9},{9,10},{10,11},{11... | collective-permute-start | bytes 49160 | tf_op jit(solution)/shard_map/ppermute | solution.py:24
  88.3 1.3 collective-permute-start.22
  89.6 4.5 %collective-permute-start.23 = (f32[2,1,2048]{2,1,0:T(1,128)S(1)}, f32[2,1,2048]{2,1,0:T(1,128)S(1)}, u32[]{:S(2)}, u32[]{:S(2)}) collective-permute-start(f32[2,1,2048]{2,1,0:T(1,128)S(1)} %get-tuple-element.108), channel_id=1, source_target_pairs={{0,1},{1,2},{2,3},{3,4},{4,5},{5,6},{6,7},{8,9},{9,10},{10,11},{11... | collective-permute-start | bytes 49160 | tf_op jit(solution)/shard_map/ppermute | solution.py:24
  95.4 1.4 broadcast_divide_fusion
  97.7 3.6 %collective-permute-start.24 = (f32[1,2048]{1,0:T(1,128)S(1)}, f32[1,2048]{1,0:T(1,128)S(1)}, u32[]{:S(2)}, u32[]{:S(2)}) collective-permute-start(f32[1,2048]{1,0:T(1,128)S(1)} %get-tuple-element.111), channel_id=1, source_target_pairs={{0,1},{1,2},{2,3},{3,4},{4,5},{5,6},{6,7},{8,9},{9,10},{10,11},{11... | collective-permute-start | bytes 24584 | tf_op jit(solution)/shard_map/ppermute | solution.py:24
  101.3 1.3 collective-permute-start.26
  102.6 40.1 %all-reduce.25.cloned.1.call-done = f32[16,2048]{1,0:T(8,128)} async-done(((f32[16,2048]{1,0:T(8,128)}), f32[16,2048]{1,0:T(8,128)}) %all-reduce.25.cloned.1.call-update) | async-done | bytes 131088 | tf_op jit(solution)/shard_map/psum | solution.py:113
  142.7 0.9 add.321
  143.7 1.3 collective-permute-start.25
  145.0 1.3 collective-permute-start.27
  146.5 3.3 %collective-permute-done.27 = f32[1,2048]{1,0:T(1,128)S(1)} collective-permute-done((f32[1,2048]{1,0:T(1,128)S(1)}, f32[1,2048]{1,0:T(1,128)S(1)}, u32[]{:S(2)}, u32[]{:S(2)}) %collective-permute-start.27) | collective-permute-done | bytes 8224 | tf_op jit(solution)/shard_map/ppermute | solution.py:26
  150.8 1.4 pad_maximum_fusion.38
  152.1 16.0 %psum.22 = f32[2]{0:T(128)S(1)} all-reduce(f32[2]{0:T(128)S(1)} %pad_maximum_fusion.38), channel_id=1, replica_groups=mesh['cond'=4,'space'=8] {'space'}, use_global_device_ids=true, to_apply=%region_5.6 | all-reduce | flops 2 | bytes 16 | tf_op jit(solution)/shard_map/psum | solution.py:82
  170.1 1.3 collective-permute-start.28
  171.4 1.3 collective-permute-start.29
  172.7 1.8 collective-permute-done.29
  174.6 0.9 multiply_reduce_fusion
  175.5 1.4 pad_maximum_fusion.39
  177.6 14.5 %psum.23 = f32[2]{0:T(128)S(1)} all-reduce(f32[2]{0:T(128)S(1)} %pad_maximum_fusion.39), channel_id=1, replica_groups=mesh['cond'=4,'space'=8] {'space'}, use_global_device_ids=true, to_apply=%region_8.9 | all-reduce | flops 2 | bytes 16 | tf_op jit(solution)/shard_map/psum | solution.py:82
  (117 shorter events, 15.9 us)
Async XLA Ops:
  7.2 135.5 %all-reduce.25.cloned.1.call-start = ((), (), s32[]{:S(2)}) async-start(), calls=%async_computation | async-start | bytes 262144 | tf_op jit(solution)/shard_map/psum | solution.py:113
  8.4 3.9 %copy-start.4 = (s32[2,16,2048]{2,1,0:T(8,128)S(1)}, s32[2,16,2048]{2,1,0:T(8,128)}, u32[]{:S(2)}) copy-start(s32[2,16,2048]{2,1,0:T(8,128)} %param.10) | copy-start | bytes 786436
  8.4 3.9 %collective-permute-start = (f32[2,2,1,2048]{3,2,0,1:T(1,128)S(1)}, f32[2,2,1,2048]{3,2,0,1:T(1,128)S(1)}, u32[]{:S(2)}, u32[]{:S(2)}) collective-permute-start(f32[2,2,1,2048]{3,2,0,1:T(1,128)S(1)} %get-tuple-element.99), channel_id=1, source_target_pairs={{0,1},{1,2},{2,3},{3,4},{4,5},{5,6},{6,7},{8,9},{9,10},{10,11},{11... | collective-permute-start | bytes 98312 | tf_op jit(solution)/shard_map/ppermute | solution.py:24
  11.0 5.3 %collective-permute-start.1 = (f32[2,2,1,2048]{3,2,0,1:T(1,128)S(1)}, f32[2,2,1,2048]{3,2,0,1:T(1,128)S(1)}, u32[]{:S(2)}, u32[]{:S(2)}) collective-permute-start(f32[2,2,1,2048]{3,2,0,1:T(1,128)S(1)} %get-tuple-element.100), channel_id=1, source_target_pairs={{1,0},{2,1},{3,2},{4,3},{5,4},{6,5},{7,6},{9,8},{10,9},{11,10},{12... | collective-permute-start | bytes 98312 | tf_op jit(solution)/shard_map/ppermute | solution.py:26
  16.4 1.1 copy-start
  16.4 1.3 copy-start.1
  16.4 1.3 copy-start.2
  18.3 5.8 %collective-permute-start.2 = (f32[2,2,1,2048]{3,2,0,1:T(1,128)S(1)}, f32[2,2,1,2048]{3,2,0,1:T(1,128)S(1)}, u32[]{:S(2)}, u32[]{:S(2)}) collective-permute-start(f32[2,2,1,2048]{3,2,0,1:T(1,128)S(1)} %get-tuple-element.97), channel_id=1, source_target_pairs={{0,1},{1,2},{2,3},{3,4},{4,5},{5,6},{6,7},{8,9},{9,10},{10,11},{11... | collective-permute-start | bytes 98312 | tf_op jit(solution)/shard_map/ppermute | solution.py:24
  22.9 3.1 %collective-permute-start.3 = (f32[2,2,1,2048]{3,2,0,1:T(1,128)S(1)}, f32[2,2,1,2048]{3,2,0,1:T(1,128)S(1)}, u32[]{:S(2)}, u32[]{:S(2)}) collective-permute-start(f32[2,2,1,2048]{3,2,0,1:T(1,128)S(1)} %get-tuple-element.98), channel_id=1, source_target_pairs={{1,0},{2,1},{3,2},{4,3},{5,4},{6,5},{7,6},{9,8},{10,9},{11,10},{12... | collective-permute-start | bytes 98312 | tf_op jit(solution)/shard_map/ppermute | solution.py:26
  26.9 5.4 %copy-start.6 = (s32[16,2048]{1,0:T(8,128)S(1)}, s32[16,2048]{1,0:T(8,128)}, u32[]{:S(2)}) copy-start(s32[16,2048]{1,0:T(8,128)} %param.12) | copy-start | bytes 393220
  27.0 5.4 %collective-permute-start.4 = (f32[2,2,1,2048]{3,2,0,1:T(1,128)S(1)}, f32[2,2,1,2048]{3,2,0,1:T(1,128)S(1)}, u32[]{:S(2)}, u32[]{:S(2)}) collective-permute-start(f32[2,2,1,2048]{3,2,0,1:T(1,128)S(1)} %get-tuple-element.95), channel_id=1, source_target_pairs={{0,1},{1,2},{2,3},{3,4},{4,5},{5,6},{6,7},{8,9},{9,10},{10,11},{11... | collective-permute-start | bytes 98312 | tf_op jit(solution)/shard_map/ppermute | solution.py:24
  31.0 3.1 %collective-permute-start.5 = (f32[2,2,1,2048]{3,2,0,1:T(1,128)S(1)}, f32[2,2,1,2048]{3,2,0,1:T(1,128)S(1)}, u32[]{:S(2)}, u32[]{:S(2)}) collective-permute-start(f32[2,2,1,2048]{3,2,0,1:T(1,128)S(1)} %get-tuple-element.96), channel_id=1, source_target_pairs={{1,0},{2,1},{3,2},{4,3},{5,4},{6,5},{7,6},{9,8},{10,9},{11,10},{12... | collective-permute-start | bytes 98312 | tf_op jit(solution)/shard_map/ppermute | solution.py:26
  35.2 5.4 %collective-permute-start.6 = (f32[2,2,1,2048]{3,2,0,1:T(1,128)S(1)}, f32[2,2,1,2048]{3,2,0,1:T(1,128)S(1)}, u32[]{:S(2)}, u32[]{:S(2)}) collective-permute-start(f32[2,2,1,2048]{3,2,0,1:T(1,128)S(1)} %get-tuple-element.93), channel_id=1, source_target_pairs={{0,1},{1,2},{2,3},{3,4},{4,5},{5,6},{6,7},{8,9},{9,10},{10,11},{11... | collective-permute-start | bytes 98312 | tf_op jit(solution)/shard_map/ppermute | solution.py:24
  39.3 3.1 %collective-permute-start.7 = (f32[2,2,1,2048]{3,2,0,1:T(1,128)S(1)}, f32[2,2,1,2048]{3,2,0,1:T(1,128)S(1)}, u32[]{:S(2)}, u32[]{:S(2)}) collective-permute-start(f32[2,2,1,2048]{3,2,0,1:T(1,128)S(1)} %get-tuple-element.94), channel_id=1, source_target_pairs={{1,0},{2,1},{3,2},{4,3},{5,4},{6,5},{7,6},{9,8},{10,9},{11,10},{12... | collective-permute-start | bytes 98312 | tf_op jit(solution)/shard_map/ppermute | solution.py:26
  43.6 5.4 %collective-permute-start.8 = (f32[2,2,1,2048]{3,2,0,1:T(1,128)S(1)}, f32[2,2,1,2048]{3,2,0,1:T(1,128)S(1)}, u32[]{:S(2)}, u32[]{:S(2)}) collective-permute-start(f32[2,2,1,2048]{3,2,0,1:T(1,128)S(1)} %get-tuple-element.91), channel_id=1, source_target_pairs={{0,1},{1,2},{2,3},{3,4},{4,5},{5,6},{6,7},{8,9},{9,10},{10,11},{11... | collective-permute-start | bytes 98312 | tf_op jit(solution)/shard_map/ppermute | solution.py:24
  47.6 3.1 %collective-permute-start.9 = (f32[2,2,1,2048]{3,2,0,1:T(1,128)S(1)}, f32[2,2,1,2048]{3,2,0,1:T(1,128)S(1)}, u32[]{:S(2)}, u32[]{:S(2)}) collective-permute-start(f32[2,2,1,2048]{3,2,0,1:T(1,128)S(1)} %get-tuple-element.92), channel_id=1, source_target_pairs={{1,0},{2,1},{3,2},{4,3},{5,4},{6,5},{7,6},{9,8},{10,9},{11,10},{12... | collective-permute-start | bytes 98312 | tf_op jit(solution)/shard_map/ppermute | solution.py:26
  52.1 10.4 %collective-permute-start.10 = (f32[2,2,1,2048]{3,2,0,1:T(1,128)S(1)}, f32[2,2,1,2048]{3,2,0,1:T(1,128)S(1)}, u32[]{:S(2)}, u32[]{:S(2)}) collective-permute-start(f32[2,2,1,2048]{3,2,0,1:T(1,128)S(1)} %get-tuple-element.89), channel_id=1, source_target_pairs={{0,1},{1,2},{2,3},{3,4},{4,5},{5,6},{6,7},{8,9},{9,10},{10,11},{11... | collective-permute-start | bytes 98312 | tf_op jit(solution)/shard_map/ppermute | solution.py:24
  56.1 6.3 %collective-permute-start.11 = (f32[2,2,1,2048]{3,2,0,1:T(1,128)S(1)}, f32[2,2,1,2048]{3,2,0,1:T(1,128)S(1)}, u32[]{:S(2)}, u32[]{:S(2)}) collective-permute-start(f32[2,2,1,2048]{3,2,0,1:T(1,128)S(1)} %get-tuple-element.90), channel_id=1, source_target_pairs={{1,0},{2,1},{3,2},{4,3},{5,4},{6,5},{7,6},{9,8},{10,9},{11,10},{12... | collective-permute-start | bytes 98312 | tf_op jit(solution)/shard_map/ppermute | solution.py:26
  57.5 26.5 %collective-permute-start.16 = (f32[2,1,2048]{2,1,0:T(1,128)S(1)}, f32[2,1,2048]{2,1,0:T(1,128)S(1)}, u32[]{:S(2)}, u32[]{:S(2)}) collective-permute-start(f32[2,1,2048]{2,1,0:T(1,128)S(1)} %get-tuple-element.101), channel_id=1, source_target_pairs={{1,0},{2,1},{3,2},{4,3},{5,4},{6,5},{7,6},{9,8},{10,9},{11,10},{12... | collective-permute-start | bytes 49160 | tf_op jit(solution)/shard_map/ppermute | solution.py:26
  58.8 29.5 %collective-permute-start.17 = (f32[2,1,2048]{2,1,0:T(1,128)S(1)}, f32[2,1,2048]{2,1,0:T(1,128)S(1)}, u32[]{:S(2)}, u32[]{:S(2)}) collective-permute-start(f32[2,1,2048]{2,1,0:T(1,128)S(1)} %get-tuple-element.102), channel_id=1, source_target_pairs={{0,1},{1,2},{2,3},{3,4},{4,5},{5,6},{6,7},{8,9},{9,10},{10,11},{11... | collective-permute-start | bytes 49160 | tf_op jit(solution)/shard_map/ppermute | solution.py:24
  63.9 6.3 %collective-permute-start.12 = (f32[2,2,1,2048]{3,2,0,1:T(1,128)S(1)}, f32[2,2,1,2048]{3,2,0,1:T(1,128)S(1)}, u32[]{:S(2)}, u32[]{:S(2)}) collective-permute-start(f32[2,2,1,2048]{3,2,0,1:T(1,128)S(1)} %get-tuple-element.87), channel_id=1, source_target_pairs={{0,1},{1,2},{2,3},{3,4},{4,5},{5,6},{6,7},{8,9},{9,10},{10,11},{11... | collective-permute-start | bytes 98312 | tf_op jit(solution)/shard_map/ppermute | solution.py:24
  67.5 3.1 %collective-permute-start.13 = (f32[2,2,1,2048]{3,2,0,1:T(1,128)S(1)}, f32[2,2,1,2048]{3,2,0,1:T(1,128)S(1)}, u32[]{:S(2)}, u32[]{:S(2)}) collective-permute-start(f32[2,2,1,2048]{3,2,0,1:T(1,128)S(1)} %get-tuple-element.88), channel_id=1, source_target_pairs={{1,0},{2,1},{3,2},{4,3},{5,4},{6,5},{7,6},{9,8},{10,9},{11,10},{12... | collective-permute-start | bytes 98312 | tf_op jit(solution)/shard_map/ppermute | solution.py:26
  68.9 20.7 %collective-permute-start.18 = (f32[2,1,2048]{2,1,0:T(1,128)S(1)}, f32[2,1,2048]{2,1,0:T(1,128)S(1)}, u32[]{:S(2)}, u32[]{:S(2)}) collective-permute-start(f32[2,1,2048]{2,1,0:T(1,128)S(1)} %get-tuple-element.103), channel_id=1, source_target_pairs={{1,0},{2,1},{3,2},{4,3},{5,4},{6,5},{7,6},{9,8},{10,9},{11,10},{12... | collective-permute-start | bytes 49160 | tf_op jit(solution)/shard_map/ppermute | solution.py:26
  72.1 5.4 %collective-permute-start.14 = (f32[2,2,1,2048]{3,2,0,1:T(1,128)S(1)}, f32[2,2,1,2048]{3,2,0,1:T(1,128)S(1)}, u32[]{:S(2)}, u32[]{:S(2)}) collective-permute-start(f32[2,2,1,2048]{3,2,0,1:T(1,128)S(1)} %get-tuple-element.85), channel_id=1, source_target_pairs={{0,1},{1,2},{2,3},{3,4},{4,5},{5,6},{6,7},{8,9},{9,10},{10,11},{11... | collective-permute-start | bytes 98312 | tf_op jit(solution)/shard_map/ppermute | solution.py:24
  76.2 4.8 %collective-permute-start.15 = (f32[2,2,1,2048]{3,2,0,1:T(1,128)S(1)}, f32[2,2,1,2048]{3,2,0,1:T(1,128)S(1)}, u32[]{:S(2)}, u32[]{:S(2)}) collective-permute-start(f32[2,2,1,2048]{3,2,0,1:T(1,128)S(1)} %get-tuple-element.86), channel_id=1, source_target_pairs={{1,0},{2,1},{3,2},{4,3},{5,4},{6,5},{7,6},{9,8},{10,9},{11,10},{12... | collective-permute-start | bytes 98312 | tf_op jit(solution)/shard_map/ppermute | solution.py:26
  77.5 17.2 %collective-permute-start.19 = (f32[2,1,2048]{2,1,0:T(1,128)S(1)}, f32[2,1,2048]{2,1,0:T(1,128)S(1)}, u32[]{:S(2)}, u32[]{:S(2)}) collective-permute-start(f32[2,1,2048]{2,1,0:T(1,128)S(1)} %get-tuple-element.104), channel_id=1, source_target_pairs={{0,1},{1,2},{2,3},{3,4},{4,5},{5,6},{6,7},{8,9},{9,10},{10,11},{11... | collective-permute-start | bytes 49160 | tf_op jit(solution)/shard_map/ppermute | solution.py:24
  81.0 13.8 %collective-permute-start.20 = (f32[2,1,2048]{2,1,0:T(1,128)S(1)}, f32[2,1,2048]{2,1,0:T(1,128)S(1)}, u32[]{:S(2)}, u32[]{:S(2)}) collective-permute-start(f32[2,1,2048]{2,1,0:T(1,128)S(1)} %get-tuple-element.105), channel_id=1, source_target_pairs={{1,0},{2,1},{3,2},{4,3},{5,4},{6,5},{7,6},{9,8},{10,9},{11,10},{12... | collective-permute-start | bytes 49160 | tf_op jit(solution)/shard_map/ppermute | solution.py:26
  84.0 10.8 %collective-permute-start.21 = (f32[2,1,2048]{2,1,0:T(1,128)S(1)}, f32[2,1,2048]{2,1,0:T(1,128)S(1)}, u32[]{:S(2)}, u32[]{:S(2)}) collective-permute-start(f32[2,1,2048]{2,1,0:T(1,128)S(1)} %get-tuple-element.106), channel_id=1, source_target_pairs={{0,1},{1,2},{2,3},{3,4},{4,5},{5,6},{6,7},{8,9},{9,10},{10,11},{11... | collective-permute-start | bytes 49160 | tf_op jit(solution)/shard_map/ppermute | solution.py:24
  88.3 5.8 %copy-start.7 = (s32[8]{0:T(128)S(1)}, s32[8]{0:T(128)}, u32[]{:S(2)}) copy-start(s32[8]{0:T(128)} %param.13) | copy-start | bytes 100
  88.3 6.5 %collective-permute-start.22 = (f32[2,1,2048]{2,1,0:T(1,128)S(1)}, f32[2,1,2048]{2,1,0:T(1,128)S(1)}, u32[]{:S(2)}, u32[]{:S(2)}) collective-permute-start(f32[2,1,2048]{2,1,0:T(1,128)S(1)} %get-tuple-element.107), channel_id=1, source_target_pairs={{1,0},{2,1},{3,2},{4,3},{5,4},{6,5},{7,6},{9,8},{10,9},{11,10},{12... | collective-permute-start | bytes 49160 | tf_op jit(solution)/shard_map/ppermute | solution.py:26
  89.6 5.2 %collective-permute-start.23 = (f32[2,1,2048]{2,1,0:T(1,128)S(1)}, f32[2,1,2048]{2,1,0:T(1,128)S(1)}, u32[]{:S(2)}, u32[]{:S(2)}) collective-permute-start(f32[2,1,2048]{2,1,0:T(1,128)S(1)} %get-tuple-element.108), channel_id=1, source_target_pairs={{0,1},{1,2},{2,3},{3,4},{4,5},{5,6},{6,7},{8,9},{9,10},{10,11},{11... | collective-permute-start | bytes 49160 | tf_op jit(solution)/shard_map/ppermute | solution.py:24
  95.4 47.3 %copy-start.5 = (f32[16,2048]{1,0:T(8,128)S(1)}, f32[16,2048]{1,0:T(8,128)}, u32[]{:S(2)}) copy-start(f32[16,2048]{1,0:T(8,128)} %param.14) | copy-start | bytes 393220
  96.8 0.9 copy-start.3
  97.7 48.6 %collective-permute-start.24 = (f32[1,2048]{1,0:T(1,128)S(1)}, f32[1,2048]{1,0:T(1,128)S(1)}, u32[]{:S(2)}, u32[]{:S(2)}) collective-permute-start(f32[1,2048]{1,0:T(1,128)S(1)} %get-tuple-element.111), channel_id=1, source_target_pairs={{0,1},{1,2},{2,3},{3,4},{4,5},{5,6},{6,7},{8,9},{9,10},{10,11},{11... | collective-permute-start | bytes 24584 | tf_op jit(solution)/shard_map/ppermute | solution.py:24
  101.3 44.9 %collective-permute-start.26 = (f32[1,2048]{1,0:T(1,128)S(1)}, f32[1,2048]{1,0:T(1,128)S(1)}, u32[]{:S(2)}, u32[]{:S(2)}) collective-permute-start(f32[1,2048]{1,0:T(1,128)S(1)} %get-tuple-element.112), channel_id=1, source_target_pairs={{1,0},{2,1},{3,2},{4,3},{5,4},{6,5},{7,6},{9,8},{10,9},{11,10},{12... | collective-permute-start | bytes 24584 | tf_op jit(solution)/shard_map/ppermute | solution.py:26
  143.7 2.8 %collective-permute-start.25 = (f32[1,2048]{1,0:T(1,128)S(1)}, f32[1,2048]{1,0:T(1,128)S(1)}, u32[]{:S(2)}, u32[]{:S(2)}) collective-permute-start(f32[1,2048]{1,0:T(1,128)S(1)} %get-tuple-element.113), channel_id=1, source_target_pairs={{0,1},{1,2},{2,3},{3,4},{4,5},{5,6},{6,7},{8,9},{9,10},{10,11},{11... | collective-permute-start | bytes 24584 | tf_op jit(solution)/shard_map/ppermute | solution.py:24
  145.0 4.8 %collective-permute-start.27 = (f32[1,2048]{1,0:T(1,128)S(1)}, f32[1,2048]{1,0:T(1,128)S(1)}, u32[]{:S(2)}, u32[]{:S(2)}) collective-permute-start(f32[1,2048]{1,0:T(1,128)S(1)} %get-tuple-element.114), channel_id=1, source_target_pairs={{1,0},{2,1},{3,2},{4,3},{5,4},{6,5},{7,6},{9,8},{10,9},{11,10},{12... | collective-permute-start | bytes 24584 | tf_op jit(solution)/shard_map/ppermute | solution.py:26
  170.1 2.6 %collective-permute-start.28 = (f32[1,2048]{1,0:T(1,128)S(1)}, f32[1,2048]{1,0:T(1,128)S(1)}, u32[]{:S(2)}, u32[]{:S(2)}) collective-permute-start(f32[1,2048]{1,0:T(1,128)S(1)} %get-tuple-element.109), channel_id=1, source_target_pairs={{0,1},{1,2},{2,3},{3,4},{4,5},{5,6},{6,7},{8,9},{9,10},{10,11},{11... | collective-permute-start | bytes 24584 | tf_op jit(solution)/shard_map/ppermute | solution.py:24
  171.4 3.1 %collective-permute-start.29 = (f32[1,2048]{1,0:T(1,128)S(1)}, f32[1,2048]{1,0:T(1,128)S(1)}, u32[]{:S(2)}, u32[]{:S(2)}) collective-permute-start(f32[1,2048]{1,0:T(1,128)S(1)} %get-tuple-element.110), channel_id=1, source_target_pairs={{1,0},{2,1},{3,2},{4,3},{5,4},{6,5},{7,6},{9,8},{10,9},{11,10},{12... | collective-permute-start | bytes 24584 | tf_op jit(solution)/shard_map/ppermute | solution.py:26
Sparse Core Ops, SparseCore 0:
  96.9 45.7 all-reduce.24
where the time goes:
time: 206 us; the launch traced here: 205 us
  starting transfers between devices  72.4 us (35%)
  waiting for transfers between devices  56.7 us (28%)
  blocking collectives  30.5 us (15%)
  between operations  20.6 us (10%)
  other arithmetic  19.7 us (10%)
  local copies, waits for them, and re-layouts  4.73 us (2%)
    ppermute x15, starting transfers between devices, with_halo(): lax.ppermute(tail, axis, [(i, (i + 1) % count) for i in range(ends)])  53 us
    psum x1, waiting for transfers between devices, local(): portion = lax.psum(own_part, 'cond')  40.1 us
    psum x2, blocking collectives, reduce_all(): return lax.psum(values, 'space')  30.5 us
    ppermute x15, starting transfers between devices, with_halo(): lax.ppermute(head, axis, [((i + 1) % count, i) for i in range(ends)])  19.4 us
    ppermute x15, waiting for transfers between devices, with_halo(): lax.ppermute(head, axis, [((i + 1) % count, i) for i in range(ends)])  16.6 us
  transfers between devices with their start and end apart: 31, of which 9 were waited for; matrix products, arithmetic and copies ran while one was open for 3% of the time, Pallas kernels for 0%

commit v1 on v0

--- a/solution.py
+++ b/solution.py
@@ -2,6 +2,7 @@
 import jax.numpy as jnp
 from jax import lax
 from jax.sharding import PartitionSpec as P
+from jax.lax import all_gather
 
 STEPS = 4
 ITERS = 2
@@ -110,7 +111,7 @@
         weight_all, lax.axis_index("cond") * cond_here, cond_here
     )
     own_part = jnp.sum(weight_mine[:, None, None] * bed_change, 0) / jnp.sum(weight_all)
-    portion = lax.psum(own_part, "cond")
+    portion = all_gather(own_part, axis_name="cond").sum(axis=0)
     padded = rim_cells(diffusivity)
     centre = padded[1:-1, 1:-1]
     coefs = [centre * other / (centre + other) for other in neighbours(padded)]

time: 206 us -> 162 us (0.79)
  waiting for transfers between devices: 56.7 us -> 16.3 us
  between operations: 20.6 us -> 7.37 us
  blocking collectives: 30.5 us -> 41.7 us
    psum x1 -> x0, waiting for transfers between devices: 40.1 us -> none  [local(): portion = lax.psum(own_part, 'cond')]
    all_gather x0 -> x1, blocking collectives: none -> 11.4 us  [local(): portion = all_gather(own_part, axis_name='cond').sum(axis=0)]
  transfers between devices with their start and end apart: 31 -> 30, of which waited for: 9 -> 8; matrix products, arithmetic and copies ran while one was open for 3% -> 4% of each run, Pallas kernels for 0% -> 0%
where the time goes in v1:
time: 162 us; the launch traced here: 161 us
  starting transfers between devices  72.5 us (45%)
  blocking collectives  41.7 us (26%)
  other arithmetic  18.1 us (11%)
  waiting for transfers between devices  16.3 us (10%)
  between operations  7.37 us (5%)
  local copies, waits for them, and re-layouts  4.72 us (3%)
    ppermute x15, starting transfers between devices, with_halo(): lax.ppermute(tail, axis, [(i, (i + 1) % count) for i in range(ends)])  53 us
    psum x2, blocking collectives, reduce_all(): return lax.psum(values, 'space')  30.2 us
    ppermute x15, starting transfers between devices, with_halo(): lax.ppermute(head, axis, [((i + 1) % count, i) for i in range(ends)])  19.6 us
    ppermute x15, waiting for transfers between devices, with_halo(): lax.ppermute(head, axis, [((i + 1) % count, i) for i in range(ends)])  16.3 us
    all_gather x1, blocking collectives, local(): portion = all_gather(own_part, axis_name='cond').sum(axis=0)  11.4 us
  transfers between devices with their start and end apart: 30, of which 8 were waited for; matrix products, arithmetic and copies ran while one was open for 4% of the time, Pallas kernels for 0%

profile of v1, /device:TPU:0, one launch (start us, length us, event | category | flops | bytes accessed | tf_op | source)
XLA Modules:
  0.0 160.7 jit_solution(3917779197810320199)
XLA Ops:
  0.6 1.2 fusion.205
  1.9 2.5 %collective-permute-start = (f32[2,2,1,2048]{3,2,0,1:T(1,128)S(1)}, f32[2,2,1,2048]{3,2,0,1:T(1,128)S(1)}, u32[]{:S(2)}, u32[]{:S(2)}) collective-permute-start(f32[2,2,1,2048]{3,2,0,1:T(1,128)S(1)} %get-tuple-element.99), channel_id=1, source_target_pairs={{0,1},{1,2},{2,3},{3,4},{4,5},{5,6},{6,7},{8,9},{9,10},{10,11},{11... | collective-permute-start | bytes 98312 | tf_op jit(solution)/shard_map/ppermute | solution.py:25
  4.4 1.3 collective-permute-start.1
  5.7 3.9 %collective-permute-done.1 = f32[2,2,1,2048]{3,2,0,1:T(1,128)S(1)} collective-permute-done((f32[2,2,1,2048]{3,2,0,1:T(1,128)S(1)}, f32[2,2,1,2048]{3,2,0,1:T(1,128)S(1)}, u32[]{:S(2)}, u32[]{:S(2)}) %collective-permute-start.1) | collective-permute-done | bytes 32800 | tf_op jit(solution)/shard_map/ppermute | solution.py:27
  9.9 1.0 copy-done
  11.8 4.5 %collective-permute-start.2 = (f32[2,2,1,2048]{3,2,0,1:T(1,128)S(1)}, f32[2,2,1,2048]{3,2,0,1:T(1,128)S(1)}, u32[]{:S(2)}, u32[]{:S(2)}) collective-permute-start(f32[2,2,1,2048]{3,2,0,1:T(1,128)S(1)} %get-tuple-element.97), channel_id=1, source_target_pairs={{0,1},{1,2},{2,3},{3,4},{4,5},{5,6},{6,7},{8,9},{9,10},{10,11},{11... | collective-permute-start | bytes 98312 | tf_op jit(solution)/shard_map/ppermute | solution.py:25
  16.3 1.3 collective-permute-start.3
  17.6 1.8 %collective-permute-done.3 = f32[2,2,1,2048]{3,2,0,1:T(1,128)S(1)} collective-permute-done((f32[2,2,1,2048]{3,2,0,1:T(1,128)S(1)}, f32[2,2,1,2048]{3,2,0,1:T(1,128)S(1)}, u32[]{:S(2)}, u32[]{:S(2)}) %collective-permute-start.3) | collective-permute-done | bytes 32800 | tf_op jit(solution)/shard_map/ppermute | solution.py:27
  20.4 4.1 %collective-permute-start.4 = (f32[2,2,1,2048]{3,2,0,1:T(1,128)S(1)}, f32[2,2,1,2048]{3,2,0,1:T(1,128)S(1)}, u32[]{:S(2)}, u32[]{:S(2)}) collective-permute-start(f32[2,2,1,2048]{3,2,0,1:T(1,128)S(1)} %get-tuple-element.95), channel_id=1, source_target_pairs={{0,1},{1,2},{2,3},{3,4},{4,5},{5,6},{6,7},{8,9},{9,10},{10,11},{11... | collective-permute-start | bytes 98312 | tf_op jit(solution)/shard_map/ppermute | solution.py:25
  24.4 1.3 collective-permute-start.5
  25.8 1.8 %collective-permute-done.5 = f32[2,2,1,2048]{3,2,0,1:T(1,128)S(1)} collective-permute-done((f32[2,2,1,2048]{3,2,0,1:T(1,128)S(1)}, f32[2,2,1,2048]{3,2,0,1:T(1,128)S(1)}, u32[]{:S(2)}, u32[]{:S(2)}) %collective-permute-start.5) | collective-permute-done | bytes 32800 | tf_op jit(solution)/shard_map/ppermute | solution.py:27
  28.6 4.1 %collective-permute-start.6 = (f32[2,2,1,2048]{3,2,0,1:T(1,128)S(1)}, f32[2,2,1,2048]{3,2,0,1:T(1,128)S(1)}, u32[]{:S(2)}, u32[]{:S(2)}) collective-permute-start(f32[2,2,1,2048]{3,2,0,1:T(1,128)S(1)} %get-tuple-element.93), channel_id=1, source_target_pairs={{0,1},{1,2},{2,3},{3,4},{4,5},{5,6},{6,7},{8,9},{9,10},{10,11},{11... | collective-permute-start | bytes 98312 | tf_op jit(solution)/shard_map/ppermute | solution.py:25
  32.7 1.3 collective-permute-start.7
  34.0 1.8 %collective-permute-done.7 = f32[2,2,1,2048]{3,2,0,1:T(1,128)S(1)} collective-permute-done((f32[2,2,1,2048]{3,2,0,1:T(1,128)S(1)}, f32[2,2,1,2048]{3,2,0,1:T(1,128)S(1)}, u32[]{:S(2)}, u32[]{:S(2)}) %collective-permute-start.7) | collective-permute-done | bytes 32800 | tf_op jit(solution)/shard_map/ppermute | solution.py:27
  37.0 4.1 %collective-permute-start.8 = (f32[2,2,1,2048]{3,2,0,1:T(1,128)S(1)}, f32[2,2,1,2048]{3,2,0,1:T(1,128)S(1)}, u32[]{:S(2)}, u32[]{:S(2)}) collective-permute-start(f32[2,2,1,2048]{3,2,0,1:T(1,128)S(1)} %get-tuple-element.91), channel_id=1, source_target_pairs={{0,1},{1,2},{2,3},{3,4},{4,5},{5,6},{6,7},{8,9},{9,10},{10,11},{11... | collective-permute-start | bytes 98312 | tf_op jit(solution)/shard_map/ppermute | solution.py:25
  41.1 1.3 collective-permute-start.9
  42.4 1.8 %collective-permute-done.9 = f32[2,2,1,2048]{3,2,0,1:T(1,128)S(1)} collective-permute-done((f32[2,2,1,2048]{3,2,0,1:T(1,128)S(1)}, f32[2,2,1,2048]{3,2,0,1:T(1,128)S(1)}, u32[]{:S(2)}, u32[]{:S(2)}) %collective-permute-start.9) | collective-permute-done | bytes 32800 | tf_op jit(solution)/shard_map/ppermute | solution.py:27
  45.5 4.1 %collective-permute-start.10 = (f32[2,2,1,2048]{3,2,0,1:T(1,128)S(1)}, f32[2,2,1,2048]{3,2,0,1:T(1,128)S(1)}, u32[]{:S(2)}, u32[]{:S(2)}) collective-permute-start(f32[2,2,1,2048]{3,2,0,1:T(1,128)S(1)} %get-tuple-element.89), channel_id=1, source_target_pairs={{0,1},{1,2},{2,3},{3,4},{4,5},{5,6},{6,7},{8,9},{9,10},{10,11},{11... | collective-permute-start | bytes 98312 | tf_op jit(solution)/shard_map/ppermute | solution.py:25
  49.6 1.3 collective-permute-start.11
  50.9 1.3 collective-permute-start.16
  52.2 3.7 %collective-permute-start.17 = (f32[2,1,2048]{2,1,0:T(1,128)S(1)}, f32[2,1,2048]{2,1,0:T(1,128)S(1)}, u32[]{:S(2)}, u32[]{:S(2)}) collective-permute-start(f32[2,1,2048]{2,1,0:T(1,128)S(1)} %get-tuple-element.102), channel_id=1, source_target_pairs={{0,1},{1,2},{2,3},{3,4},{4,5},{5,6},{6,7},{8,9},{9,10},{10,11},{11... | collective-permute-start | bytes 49160 | tf_op jit(solution)/shard_map/ppermute | solution.py:25
  57.3 3.6 %collective-permute-start.12 = (f32[2,2,1,2048]{3,2,0,1:T(1,128)S(1)}, f32[2,2,1,2048]{3,2,0,1:T(1,128)S(1)}, u32[]{:S(2)}, u32[]{:S(2)}) collective-permute-start(f32[2,2,1,2048]{3,2,0,1:T(1,128)S(1)} %get-tuple-element.87), channel_id=1, source_target_pairs={{0,1},{1,2},{2,3},{3,4},{4,5},{5,6},{6,7},{8,9},{9,10},{10,11},{11... | collective-permute-start | bytes 98312 | tf_op jit(solution)/shard_map/ppermute | solution.py:25
  61.0 1.3 collective-permute-start.13
  62.3 1.3 collective-permute-start.18
  65.6 4.1 %collective-permute-start.14 = (f32[2,2,1,2048]{3,2,0,1:T(1,128)S(1)}, f32[2,2,1,2048]{3,2,0,1:T(1,128)S(1)}, u32[]{:S(2)}, u32[]{:S(2)}) collective-permute-start(f32[2,2,1,2048]{3,2,0,1:T(1,128)S(1)} %get-tuple-element.85), channel_id=1, source_target_pairs={{0,1},{1,2},{2,3},{3,4},{4,5},{5,6},{6,7},{8,9},{9,10},{10,11},{11... | collective-permute-start | bytes 98312 | tf_op jit(solution)/shard_map/ppermute | solution.py:25
  69.6 1.3 collective-permute-start.15
  71.0 3.4 %collective-permute-start.19 = (f32[2,1,2048]{2,1,0:T(1,128)S(1)}, f32[2,1,2048]{2,1,0:T(1,128)S(1)}, u32[]{:S(2)}, u32[]{:S(2)}) collective-permute-start(f32[2,1,2048]{2,1,0:T(1,128)S(1)} %get-tuple-element.104), channel_id=1, source_target_pairs={{0,1},{1,2},{2,3},{3,4},{4,5},{5,6},{6,7},{8,9},{9,10},{10,11},{11... | collective-permute-start | bytes 49160 | tf_op jit(solution)/shard_map/ppermute | solution.py:25
  74.4 1.3 collective-permute-start.20
  76.3 0.9 fusion.19
  77.4 4.3 %collective-permute-start.21 = (f32[2,1,2048]{2,1,0:T(1,128)S(1)}, f32[2,1,2048]{2,1,0:T(1,128)S(1)}, u32[]{:S(2)}, u32[]{:S(2)}) collective-permute-start(f32[2,1,2048]{2,1,0:T(1,128)S(1)} %get-tuple-element.106), channel_id=1, source_target_pairs={{0,1},{1,2},{2,3},{3,4},{4,5},{5,6},{6,7},{8,9},{9,10},{10,11},{11... | collective-permute-start | bytes 49160 | tf_op jit(solution)/shard_map/ppermute | solution.py:25
  81.7 1.3 collective-permute-start.22
  83.0 4.3 %collective-permute-start.23 = (f32[2,1,2048]{2,1,0:T(1,128)S(1)}, f32[2,1,2048]{2,1,0:T(1,128)S(1)}, u32[]{:S(2)}, u32[]{:S(2)}) collective-permute-start(f32[2,1,2048]{2,1,0:T(1,128)S(1)} %get-tuple-element.108), channel_id=1, source_target_pairs={{0,1},{1,2},{2,3},{3,4},{4,5},{5,6},{6,7},{8,9},{9,10},{10,11},{11... | collective-permute-start | bytes 49160 | tf_op jit(solution)/shard_map/ppermute | solution.py:25
  88.0 3.6 %collective-permute-start.24 = (f32[1,2048]{1,0:T(1,128)S(1)}, f32[1,2048]{1,0:T(1,128)S(1)}, u32[]{:S(2)}, u32[]{:S(2)}) collective-permute-start(f32[1,2048]{1,0:T(1,128)S(1)} %get-tuple-element.111), channel_id=1, source_target_pairs={{0,1},{1,2},{2,3},{3,4},{4,5},{5,6},{6,7},{8,9},{9,10},{10,11},{11... | collective-permute-start | bytes 24584 | tf_op jit(solution)/shard_map/ppermute | solution.py:25
  91.7 1.5 collective-permute-start.26
  94.5 11.4 %all-gather = f32[64,2048]{1,0:T(8,128)S(1)} all-gather(f32[16,2048]{1,0:T(8,128)S(1)} %broadcast_divide_fusion), channel_id=2, replica_groups=mesh['cond'=4,'space'=8] {'cond'}, dimensions={0}, use_global_device_ids=true | all-gather | bytes 655360 | tf_op jit(solution)/shard_map/all_gather | solution.py:114
  105.9 0.9 copy-done.5
  106.8 1.4 collective-permute-start.25
  108.3 1.3 collective-permute-start.27
  109.8 3.0 %collective-permute-done.27 = f32[1,2048]{1,0:T(1,128)S(1)} collective-permute-done((f32[1,2048]{1,0:T(1,128)S(1)}, f32[1,2048]{1,0:T(1,128)S(1)}, u32[]{:S(2)}, u32[]{:S(2)}) %collective-permute-start.27) | collective-permute-done | bytes 8224 | tf_op jit(solution)/shard_map/ppermute | solution.py:27
  113.0 0.9 multiply_reduce_fusion.2
  113.8 1.4 pad_maximum_fusion.38
  115.2 16.0 %psum.14 = f32[2]{0:T(128)S(1)} all-reduce(f32[2]{0:T(128)S(1)} %pad_maximum_fusion.38), channel_id=1, replica_groups=mesh['cond'=4,'space'=8] {'space'}, use_global_device_ids=true, to_apply=%region_5.6 | all-reduce | flops 2 | bytes 16 | tf_op jit(solution)/shard_map/psum | solution.py:83
  133.1 1.3 collective-permute-start.28
  134.4 1.3 collective-permute-start.29
  135.7 1.8 %collective-permute-done.29 = f32[1,2048]{1,0:T(1,128)S(1)} collective-permute-done((f32[1,2048]{1,0:T(1,128)S(1)}, f32[1,2048]{1,0:T(1,128)S(1)}, u32[]{:S(2)}, u32[]{:S(2)}) %collective-permute-start.29) | collective-permute-done | bytes 8224 | tf_op jit(solution)/shard_map/ppermute | solution.py:27
  137.6 0.9 multiply_reduce_fusion
  138.6 1.4 pad_maximum_fusion.39
  140.7 14.2 %psum.15 = f32[2]{0:T(128)S(1)} all-reduce(f32[2]{0:T(128)S(1)} %pad_maximum_fusion.39), channel_id=1, replica_groups=mesh['cond'=4,'space'=8] {'space'}, use_global_device_ids=true, to_apply=%region_8.9 | all-reduce | flops 2 | bytes 16 | tf_op jit(solution)/shard_map/psum | solution.py:83
  (116 shorter events, 14.8 us)
Async XLA Ops:
  1.8 3.9 %copy-start.4 = (s32[2,16,2048]{2,1,0:T(8,128)S(1)}, s32[2,16,2048]{2,1,0:T(8,128)}, u32[]{:S(2)}) copy-start(s32[2,16,2048]{2,1,0:T(8,128)} %param.10) | copy-start | bytes 786436
  1.9 3.9 %collective-permute-start = (f32[2,2,1,2048]{3,2,0,1:T(1,128)S(1)}, f32[2,2,1,2048]{3,2,0,1:T(1,128)S(1)}, u32[]{:S(2)}, u32[]{:S(2)}) collective-permute-start(f32[2,2,1,2048]{3,2,0,1:T(1,128)S(1)} %get-tuple-element.99), channel_id=1, source_target_pairs={{0,1},{1,2},{2,3},{3,4},{4,5},{5,6},{6,7},{8,9},{9,10},{10,11},{11... | collective-permute-start | bytes 98312 | tf_op jit(solution)/shard_map/ppermute | solution.py:25
  4.4 5.3 %collective-permute-start.1 = (f32[2,2,1,2048]{3,2,0,1:T(1,128)S(1)}, f32[2,2,1,2048]{3,2,0,1:T(1,128)S(1)}, u32[]{:S(2)}, u32[]{:S(2)}) collective-permute-start(f32[2,2,1,2048]{3,2,0,1:T(1,128)S(1)} %get-tuple-element.100), channel_id=1, source_target_pairs={{1,0},{2,1},{3,2},{4,3},{5,4},{6,5},{7,6},{9,8},{10,9},{11,10},{12... | collective-permute-start | bytes 98312 | tf_op jit(solution)/shard_map/ppermute | solution.py:27
  9.8 1.1 copy-start
  9.8 1.3 copy-start.1
  9.8 1.3 copy-start.2
  11.8 5.8 %collective-permute-start.2 = (f32[2,2,1,2048]{3,2,0,1:T(1,128)S(1)}, f32[2,2,1,2048]{3,2,0,1:T(1,128)S(1)}, u32[]{:S(2)}, u32[]{:S(2)}) collective-permute-start(f32[2,2,1,2048]{3,2,0,1:T(1,128)S(1)} %get-tuple-element.97), channel_id=1, source_target_pairs={{0,1},{1,2},{2,3},{3,4},{4,5},{5,6},{6,7},{8,9},{9,10},{10,11},{11... | collective-permute-start | bytes 98312 | tf_op jit(solution)/shard_map/ppermute | solution.py:25
  16.3 3.1 %collective-permute-start.3 = (f32[2,2,1,2048]{3,2,0,1:T(1,128)S(1)}, f32[2,2,1,2048]{3,2,0,1:T(1,128)S(1)}, u32[]{:S(2)}, u32[]{:S(2)}) collective-permute-start(f32[2,2,1,2048]{3,2,0,1:T(1,128)S(1)} %get-tuple-element.98), channel_id=1, source_target_pairs={{1,0},{2,1},{3,2},{4,3},{5,4},{6,5},{7,6},{9,8},{10,9},{11,10},{12... | collective-permute-start | bytes 98312 | tf_op jit(solution)/shard_map/ppermute | solution.py:27
  20.3 5.4 %copy-start.6 = (s32[16,2048]{1,0:T(8,128)S(1)}, s32[16,2048]{1,0:T(8,128)}, u32[]{:S(2)}) copy-start(s32[16,2048]{1,0:T(8,128)} %param.12) | copy-start | bytes 393220
  20.4 5.4 %collective-permute-start.4 = (f32[2,2,1,2048]{3,2,0,1:T(1,128)S(1)}, f32[2,2,1,2048]{3,2,0,1:T(1,128)S(1)}, u32[]{:S(2)}, u32[]{:S(2)}) collective-permute-start(f32[2,2,1,2048]{3,2,0,1:T(1,128)S(1)} %get-tuple-element.95), channel_id=1, source_target_pairs={{0,1},{1,2},{2,3},{3,4},{4,5},{5,6},{6,7},{8,9},{9,10},{10,11},{11... | collective-permute-start | bytes 98312 | tf_op jit(solution)/shard_map/ppermute | solution.py:25
  24.4 3.1 %collective-permute-start.5 = (f32[2,2,1,2048]{3,2,0,1:T(1,128)S(1)}, f32[2,2,1,2048]{3,2,0,1:T(1,128)S(1)}, u32[]{:S(2)}, u32[]{:S(2)}) collective-permute-start(f32[2,2,1,2048]{3,2,0,1:T(1,128)S(1)} %get-tuple-element.96), channel_id=1, source_target_pairs={{1,0},{2,1},{3,2},{4,3},{5,4},{6,5},{7,6},{9,8},{10,9},{11,10},{12... | collective-permute-start | bytes 98312 | tf_op jit(solution)/shard_map/ppermute | solution.py:27
  28.6 5.4 %collective-permute-start.6 = (f32[2,2,1,2048]{3,2,0,1:T(1,128)S(1)}, f32[2,2,1,2048]{3,2,0,1:T(1,128)S(1)}, u32[]{:S(2)}, u32[]{:S(2)}) collective-permute-start(f32[2,2,1,2048]{3,2,0,1:T(1,128)S(1)} %get-tuple-element.93), channel_id=1, source_target_pairs={{0,1},{1,2},{2,3},{3,4},{4,5},{5,6},{6,7},{8,9},{9,10},{10,11},{11... | collective-permute-start | bytes 98312 | tf_op jit(solution)/shard_map/ppermute | solution.py:25
  32.7 3.1 %collective-permute-start.7 = (f32[2,2,1,2048]{3,2,0,1:T(1,128)S(1)}, f32[2,2,1,2048]{3,2,0,1:T(1,128)S(1)}, u32[]{:S(2)}, u32[]{:S(2)}) collective-permute-start(f32[2,2,1,2048]{3,2,0,1:T(1,128)S(1)} %get-tuple-element.94), channel_id=1, source_target_pairs={{1,0},{2,1},{3,2},{4,3},{5,4},{6,5},{7,6},{9,8},{10,9},{11,10},{12... | collective-permute-start | bytes 98312 | tf_op jit(solution)/shard_map/ppermute | solution.py:27
  36.9 5.4 %copy-start.3 = (f32[16,2048]{1,0:T(8,128)S(1)}, f32[16,2048]{1,0:T(8,128)}, u32[]{:S(2)}) copy-start(f32[16,2048]{1,0:T(8,128)} %param.15) | copy-start | bytes 393220
  37.0 5.4 %collective-permute-start.8 = (f32[2,2,1,2048]{3,2,0,1:T(1,128)S(1)}, f32[2,2,1,2048]{3,2,0,1:T(1,128)S(1)}, u32[]{:S(2)}, u32[]{:S(2)}) collective-permute-start(f32[2,2,1,2048]{3,2,0,1:T(1,128)S(1)} %get-tuple-element.91), channel_id=1, source_target_pairs={{0,1},{1,2},{2,3},{3,4},{4,5},{5,6},{6,7},{8,9},{9,10},{10,11},{11... | collective-permute-start | bytes 98312 | tf_op jit(solution)/shard_map/ppermute | solution.py:25
  41.1 3.1 %collective-permute-start.9 = (f32[2,2,1,2048]{3,2,0,1:T(1,128)S(1)}, f32[2,2,1,2048]{3,2,0,1:T(1,128)S(1)}, u32[]{:S(2)}, u32[]{:S(2)}) collective-permute-start(f32[2,2,1,2048]{3,2,0,1:T(1,128)S(1)} %get-tuple-element.92), channel_id=1, source_target_pairs={{1,0},{2,1},{3,2},{4,3},{5,4},{6,5},{7,6},{9,8},{10,9},{11,10},{12... | collective-permute-start | bytes 98312 | tf_op jit(solution)/shard_map/ppermute | solution.py:27
  45.5 10.4 %collective-permute-start.10 = (f32[2,2,1,2048]{3,2,0,1:T(1,128)S(1)}, f32[2,2,1,2048]{3,2,0,1:T(1,128)S(1)}, u32[]{:S(2)}, u32[]{:S(2)}) collective-permute-start(f32[2,2,1,2048]{3,2,0,1:T(1,128)S(1)} %get-tuple-element.89), channel_id=1, source_target_pairs={{0,1},{1,2},{2,3},{3,4},{4,5},{5,6},{6,7},{8,9},{9,10},{10,11},{11... | collective-permute-start | bytes 98312 | tf_op jit(solution)/shard_map/ppermute | solution.py:25
  49.6 6.3 %collective-permute-start.11 = (f32[2,2,1,2048]{3,2,0,1:T(1,128)S(1)}, f32[2,2,1,2048]{3,2,0,1:T(1,128)S(1)}, u32[]{:S(2)}, u32[]{:S(2)}) collective-permute-start(f32[2,2,1,2048]{3,2,0,1:T(1,128)S(1)} %get-tuple-element.90), channel_id=1, source_target_pairs={{1,0},{2,1},{3,2},{4,3},{5,4},{6,5},{7,6},{9,8},{10,9},{11,10},{12... | collective-permute-start | bytes 98312 | tf_op jit(solution)/shard_map/ppermute | solution.py:27
  50.9 26.5 %collective-permute-start.16 = (f32[2,1,2048]{2,1,0:T(1,128)S(1)}, f32[2,1,2048]{2,1,0:T(1,128)S(1)}, u32[]{:S(2)}, u32[]{:S(2)}) collective-permute-start(f32[2,1,2048]{2,1,0:T(1,128)S(1)} %get-tuple-element.101), channel_id=1, source_target_pairs={{1,0},{2,1},{3,2},{4,3},{5,4},{6,5},{7,6},{9,8},{10,9},{11,10},{12... | collective-permute-start | bytes 49160 | tf_op jit(solution)/shard_map/ppermute | solution.py:27
  52.2 29.5 %collective-permute-start.17 = (f32[2,1,2048]{2,1,0:T(1,128)S(1)}, f32[2,1,2048]{2,1,0:T(1,128)S(1)}, u32[]{:S(2)}, u32[]{:S(2)}) collective-permute-start(f32[2,1,2048]{2,1,0:T(1,128)S(1)} %get-tuple-element.102), channel_id=1, source_target_pairs={{0,1},{1,2},{2,3},{3,4},{4,5},{5,6},{6,7},{8,9},{9,10},{10,11},{11... | collective-permute-start | bytes 49160 | tf_op jit(solution)/shard_map/ppermute | solution.py:25
  57.3 6.3 %collective-permute-start.12 = (f32[2,2,1,2048]{3,2,0,1:T(1,128)S(1)}, f32[2,2,1,2048]{3,2,0,1:T(1,128)S(1)}, u32[]{:S(2)}, u32[]{:S(2)}) collective-permute-start(f32[2,2,1,2048]{3,2,0,1:T(1,128)S(1)} %get-tuple-element.87), channel_id=1, source_target_pairs={{0,1},{1,2},{2,3},{3,4},{4,5},{5,6},{6,7},{8,9},{9,10},{10,11},{11... | collective-permute-start | bytes 98312 | tf_op jit(solution)/shard_map/ppermute | solution.py:25
  61.0 3.1 %collective-permute-start.13 = (f32[2,2,1,2048]{3,2,0,1:T(1,128)S(1)}, f32[2,2,1,2048]{3,2,0,1:T(1,128)S(1)}, u32[]{:S(2)}, u32[]{:S(2)}) collective-permute-start(f32[2,2,1,2048]{3,2,0,1:T(1,128)S(1)} %get-tuple-element.88), channel_id=1, source_target_pairs={{1,0},{2,1},{3,2},{4,3},{5,4},{6,5},{7,6},{9,8},{10,9},{11,10},{12... | collective-permute-start | bytes 98312 | tf_op jit(solution)/shard_map/ppermute | solution.py:27
  62.3 20.7 %collective-permute-start.18 = (f32[2,1,2048]{2,1,0:T(1,128)S(1)}, f32[2,1,2048]{2,1,0:T(1,128)S(1)}, u32[]{:S(2)}, u32[]{:S(2)}) collective-permute-start(f32[2,1,2048]{2,1,0:T(1,128)S(1)} %get-tuple-element.103), channel_id=1, source_target_pairs={{1,0},{2,1},{3,2},{4,3},{5,4},{6,5},{7,6},{9,8},{10,9},{11,10},{12... | collective-permute-start | bytes 49160 | tf_op jit(solution)/shard_map/ppermute | solution.py:27
  65.6 5.4 %collective-permute-start.14 = (f32[2,2,1,2048]{3,2,0,1:T(1,128)S(1)}, f32[2,2,1,2048]{3,2,0,1:T(1,128)S(1)}, u32[]{:S(2)}, u32[]{:S(2)}) collective-permute-start(f32[2,2,1,2048]{3,2,0,1:T(1,128)S(1)} %get-tuple-element.85), channel_id=1, source_target_pairs={{0,1},{1,2},{2,3},{3,4},{4,5},{5,6},{6,7},{8,9},{9,10},{10,11},{11... | collective-permute-start | bytes 98312 | tf_op jit(solution)/shard_map/ppermute | solution.py:25
  69.6 4.8 %collective-permute-start.15 = (f32[2,2,1,2048]{3,2,0,1:T(1,128)S(1)}, f32[2,2,1,2048]{3,2,0,1:T(1,128)S(1)}, u32[]{:S(2)}, u32[]{:S(2)}) collective-permute-start(f32[2,2,1,2048]{3,2,0,1:T(1,128)S(1)} %get-tuple-element.86), channel_id=1, source_target_pairs={{1,0},{2,1},{3,2},{4,3},{5,4},{6,5},{7,6},{9,8},{10,9},{11,10},{12... | collective-permute-start | bytes 98312 | tf_op jit(solution)/shard_map/ppermute | solution.py:27
  71.0 17.0 %collective-permute-start.19 = (f32[2,1,2048]{2,1,0:T(1,128)S(1)}, f32[2,1,2048]{2,1,0:T(1,128)S(1)}, u32[]{:S(2)}, u32[]{:S(2)}) collective-permute-start(f32[2,1,2048]{2,1,0:T(1,128)S(1)} %get-tuple-element.104), channel_id=1, source_target_pairs={{0,1},{1,2},{2,3},{3,4},{4,5},{5,6},{6,7},{8,9},{9,10},{10,11},{11... | collective-permute-start | bytes 49160 | tf_op jit(solution)/shard_map/ppermute | solution.py:25
  74.4 17.2 %collective-permute-start.20 = (f32[2,1,2048]{2,1,0:T(1,128)S(1)}, f32[2,1,2048]{2,1,0:T(1,128)S(1)}, u32[]{:S(2)}, u32[]{:S(2)}) collective-permute-start(f32[2,1,2048]{2,1,0:T(1,128)S(1)} %get-tuple-element.105), channel_id=1, source_target_pairs={{1,0},{2,1},{3,2},{4,3},{5,4},{6,5},{7,6},{9,8},{10,9},{11,10},{12... | collective-permute-start | bytes 49160 | tf_op jit(solution)/shard_map/ppermute | solution.py:27
  77.4 15.7 %collective-permute-start.21 = (f32[2,1,2048]{2,1,0:T(1,128)S(1)}, f32[2,1,2048]{2,1,0:T(1,128)S(1)}, u32[]{:S(2)}, u32[]{:S(2)}) collective-permute-start(f32[2,1,2048]{2,1,0:T(1,128)S(1)} %get-tuple-element.106), channel_id=1, source_target_pairs={{0,1},{1,2},{2,3},{3,4},{4,5},{5,6},{6,7},{8,9},{9,10},{10,11},{11... | collective-permute-start | bytes 49160 | tf_op jit(solution)/shard_map/ppermute | solution.py:25
  81.7 5.6 %copy-start.7 = (s32[8]{0:T(128)S(1)}, s32[8]{0:T(128)}, u32[]{:S(2)}) copy-start(s32[8]{0:T(128)} %param.13) | copy-start | bytes 100
  81.7 11.4 %collective-permute-start.22 = (f32[2,1,2048]{2,1,0:T(1,128)S(1)}, f32[2,1,2048]{2,1,0:T(1,128)S(1)}, u32[]{:S(2)}, u32[]{:S(2)}) collective-permute-start(f32[2,1,2048]{2,1,0:T(1,128)S(1)} %get-tuple-element.107), channel_id=1, source_target_pairs={{1,0},{2,1},{3,2},{4,3},{5,4},{6,5},{7,6},{9,8},{10,9},{11,10},{12... | collective-permute-start | bytes 49160 | tf_op jit(solution)/shard_map/ppermute | solution.py:27
  83.0 10.1 %collective-permute-start.23 = (f32[2,1,2048]{2,1,0:T(1,128)S(1)}, f32[2,1,2048]{2,1,0:T(1,128)S(1)}, u32[]{:S(2)}, u32[]{:S(2)}) collective-permute-start(f32[2,1,2048]{2,1,0:T(1,128)S(1)} %get-tuple-element.108), channel_id=1, source_target_pairs={{0,1},{1,2},{2,3},{3,4},{4,5},{5,6},{6,7},{8,9},{9,10},{10,11},{11... | collective-permute-start | bytes 49160 | tf_op jit(solution)/shard_map/ppermute | solution.py:25
  88.0 21.6 %collective-permute-start.24 = (f32[1,2048]{1,0:T(1,128)S(1)}, f32[1,2048]{1,0:T(1,128)S(1)}, u32[]{:S(2)}, u32[]{:S(2)}) collective-permute-start(f32[1,2048]{1,0:T(1,128)S(1)} %get-tuple-element.111), channel_id=1, source_target_pairs={{0,1},{1,2},{2,3},{3,4},{4,5},{5,6},{6,7},{8,9},{9,10},{10,11},{11... | collective-permute-start | bytes 24584 | tf_op jit(solution)/shard_map/ppermute | solution.py:25
  91.7 17.9 %collective-permute-start.26 = (f32[1,2048]{1,0:T(1,128)S(1)}, f32[1,2048]{1,0:T(1,128)S(1)}, u32[]{:S(2)}, u32[]{:S(2)}) collective-permute-start(f32[1,2048]{1,0:T(1,128)S(1)} %get-tuple-element.112), channel_id=1, source_target_pairs={{1,0},{2,1},{3,2},{4,3},{5,4},{6,5},{7,6},{9,8},{10,9},{11,10},{12... | collective-permute-start | bytes 24584 | tf_op jit(solution)/shard_map/ppermute | solution.py:27
  105.9 0.9 copy-start.5
  106.8 2.9 %collective-permute-start.25 = (f32[1,2048]{1,0:T(1,128)S(1)}, f32[1,2048]{1,0:T(1,128)S(1)}, u32[]{:S(2)}, u32[]{:S(2)}) collective-permute-start(f32[1,2048]{1,0:T(1,128)S(1)} %get-tuple-element.113), channel_id=1, source_target_pairs={{0,1},{1,2},{2,3},{3,4},{4,5},{5,6},{6,7},{8,9},{9,10},{10,11},{11... | collective-permute-start | bytes 24584 | tf_op jit(solution)/shard_map/ppermute | solution.py:25
  108.3 4.5 %collective-permute-start.27 = (f32[1,2048]{1,0:T(1,128)S(1)}, f32[1,2048]{1,0:T(1,128)S(1)}, u32[]{:S(2)}, u32[]{:S(2)}) collective-permute-start(f32[1,2048]{1,0:T(1,128)S(1)} %get-tuple-element.114), channel_id=1, source_target_pairs={{1,0},{2,1},{3,2},{4,3},{5,4},{6,5},{7,6},{9,8},{10,9},{11,10},{12... | collective-permute-start | bytes 24584 | tf_op jit(solution)/shard_map/ppermute | solution.py:27
  133.1 2.6 %collective-permute-start.28 = (f32[1,2048]{1,0:T(1,128)S(1)}, f32[1,2048]{1,0:T(1,128)S(1)}, u32[]{:S(2)}, u32[]{:S(2)}) collective-permute-start(f32[1,2048]{1,0:T(1,128)S(1)} %get-tuple-element.109), channel_id=1, source_target_pairs={{0,1},{1,2},{2,3},{3,4},{4,5},{5,6},{6,7},{8,9},{9,10},{10,11},{11... | collective-permute-start | bytes 24584 | tf_op jit(solution)/shard_map/ppermute | solution.py:25
  134.4 3.1 %collective-permute-start.29 = (f32[1,2048]{1,0:T(1,128)S(1)}, f32[1,2048]{1,0:T(1,128)S(1)}, u32[]{:S(2)}, u32[]{:S(2)}) collective-permute-start(f32[1,2048]{1,0:T(1,128)S(1)} %get-tuple-element.110), channel_id=1, source_target_pairs={{1,0},{2,1},{3,2},{4,3},{5,4},{6,5},{7,6},{9,8},{10,9},{11,10},{12... | collective-permute-start | bytes 24584 | tf_op jit(solution)/shard_map/ppermute | solution.py:27
